TPU v7x, 128 devices: a whole 4x4x4 slice. The times are simulated.
128 devices in a mesh: tiles: 16 (over y, z), lag: 8 (over x, core).
Axes of the slice: x: 4, y: 4, z: 4, core: 2. Of those that a mesh axis runs over, the one named last changes fastest.
Arguments:
- spectra: bfloat16 [32, 2, 2, 128, 8192], P('tiles', None, None, None, 'lag'), may hold values from -6 to 6
- requests: int32 [16, 6], replicated, may hold values from 0 to 31, as said below
- pairs: int32 [16, 3, 2], P('tiles'), may hold values from 0 to 5, as said below
- counts: int32 [16], P('tiles'), may hold values from 2 to 3, as said below
Outputs:
- stacked_lags: float32 [48, 64, 128, 128], P('tiles', 'lag')
Inputs may be any that keep to these rules, and one draw needn't show every extreme that they name: Block b is held by index b // 2 of tiles; each row of requests names 6 blocks held by 6 different indices. Each row's 3 entries are pairs (i, j) of request slots with i < j that together use every request slot once. The first counts[d] slots of row d are live, the others give zeros; some index has 3.
All inputs are finite; a program needn't handle non-finite values.
Results may differ from a plain program's by a relative error of at most 0.012.
Values may be sent and summed in bfloat16 or wider, within the bound.
A program may use at most 128 MiB of HBM per device.

v0:
```python
import math
import jax
import jax.numpy as jnp
from jax import lax
from jax.sharding import PartitionSpec as P

F = 8192
W = 2
LAGS = 64
FBLK = 128


def phase_table(freq_first, width):
    frequencies = freq_first + jnp.arange(width, dtype=jnp.int32)
    shifts = (jnp.arange(LAGS, dtype=jnp.int32) - LAGS // 2) % F
    phase_index = frequencies[:, None] * shifts[None, :] % F
    angles = phase_index.astype(jnp.float32) * (2.0 * math.pi / F)
    return jnp.concatenate([jnp.cos(angles), -jnp.sin(angles)], axis=0).astype(jnp.bfloat16)


def cross_block(left_part, right_part):
    left_wide = left_part.astype(jnp.float32)
    right_wide = right_part.astype(jnp.float32)
    real_part = jnp.sum(
        left_wide[:, 0, :, None, :] * right_wide[:, 0, None, :, :]
        + left_wide[:, 1, :, None, :] * right_wide[:, 1, None, :, :],
        axis=0,
    )
    imag_part = jnp.sum(
        left_wide[:, 1, :, None, :] * right_wide[:, 0, None, :, :]
        - left_wide[:, 0, :, None, :] * right_wide[:, 1, None, :, :],
        axis=0,
    )
    channels = left_part.shape[2]
    return (
        jnp.concatenate([real_part, imag_part], axis=-1)
        .reshape(channels * channels, -1)
        .astype(jnp.bfloat16)
    )


def band_sum(left_block, right_block, band_first):
    channels = left_block.shape[2]
    block_count = left_block.shape[-1] // FBLK

    def block_step(running, block_index):
        offset = block_index * FBLK
        left_part = lax.dynamic_slice_in_dim(left_block, offset, FBLK, 3)
        right_part = lax.dynamic_slice_in_dim(right_block, offset, FBLK, 3)
        stacked = cross_block(left_part, right_part)
        phases = phase_table(band_first + offset, FBLK)
        return (
            running
            + lax.dot_general(
                phases, stacked, (((0,), (1,)), ((), ())), preferred_element_type=jnp.float32
            ),
            None,
        )

    running = jnp.zeros((LAGS, channels * channels), jnp.float32)
    running, unused = lax.scan(block_step, running, jnp.arange(block_count, dtype=jnp.int32))
    return running


def per_device(spectra, requests, pairs, counts):
    channels = spectra.shape[3]
    own_index = lax.axis_index("tiles")
    wanted = lax.dynamic_index_in_dim(requests, own_index, 0, keepdims=False)
    empty = jnp.zeros((wanted.shape[0],) + spectra.shape[1:], jnp.bfloat16)
    shards = lax.all_gather(spectra, "tiles", axis=0, tiled=True)
    inside = (wanted >= 0) & (wanted < shards.shape[0])
    taken = jnp.take(shards, jnp.clip(wanted, 0, shards.shape[0] - 1), axis=0)
    needed = jnp.where(inside[:, None, None, None, None], taken, empty)
    band_first = lax.axis_index("lag") * spectra.shape[-1]
    norm_factor = 1.0 / math.sqrt(2.0 * W * F)
    live_count = counts[0]
    tile_pairs = pairs[0]
    slot_total = tile_pairs.shape[0]
    terms = []
    for slot_index in range(slot_total):
        left_block = jnp.take(needed, tile_pairs[slot_index, 0], axis=0)
        right_block = jnp.take(needed, tile_pairs[slot_index, 1], axis=0)
        result = band_sum(left_block, right_block, band_first) * norm_factor
        terms.append(jnp.where(slot_index < live_count, result, jnp.zeros_like(result)))
    partial_terms = jnp.stack(terms).reshape(slot_total, LAGS, channels, channels)
    return lax.psum_scatter(
        partial_terms.astype(jnp.bfloat16), "lag", scatter_dimension=1, tiled=True
    ).astype(jnp.float32)


def solution(mesh):
    placed = (P("tiles", None, None, None, "lag"), P(), P("tiles", None, None), P("tiles"))
    return jax.shard_map(
        per_device,
        mesh=mesh,
        in_specs=placed,
        out_specs=P("tiles", "lag", None, None),
        check_vma=False,
    )
```

profile of v0, /device:TPU:1, one launch (start us, length us, event | category | flops | bytes accessed | tf_op | source)
XLA Modules:
  0.0 1019.2 jit_solution(7977212312652234884)
XLA Ops:
  22.7 187.3 %all-gather.2.cloned.1.call-done = bf16[32,2,2,128,1024]{4,3,2,1,0:T(8,128)(2,1)} async-done(((bf16[2,2,2,128,1024]{4,3,2,1,0:T(8,128)(2,1)}), bf16[32,2,2,128,1024]{4,3,2,1,0:T(8,128)(2,1)}) %all-gather.2.cloned.1.call-update) | async-done | bytes 33554448 | tf_op jit(solution)/shard_map/all_gather | solution.py:70
  221.3 236.1 %while.40 = (s32[]{:T(128)}, f32[64,16384]{1,0:T(8,128)}, s32[8]{0:T(128)S(1)}, s32[]{:T(128)}, bf16[2,2,128,1024]{3,2,1,0:T(8,128)(2,1)S(1)}, /*index=5*/bf16[2...) while((s32[]{:T(128)}, f32[64,16384]{1,0:T(8,128)}, ...), condition=%wide.region_3.5_spmd.clone, body=%wide.region_0.0_spmd.clone.sunk | while | flops 585442176 | bytes 44893884 | solution.py:61
  222.8 11.7 %add_reduce_fusion.6 = (bf16[128,128,128]{2,1,0:T(8,128)(2,1)S(1)}, bf16[128,128,128]{2,1,0:T(8,128)(2,1)}) fusion(f32[2,128,128]{2,1,0:T(8,128)S(1)} %get-tuple-element.564, f32[2,128,128]{2,1,0:T(8,128)S(1)} %get-tuple-element.566, f32[2,128,128]{2,1,0:T(8,128)S(1)} %get-tuple-element.567, f32[2,128,128]{2,1,0:T(8,128)S(1)} %get-tuple-element.568), kind=kLoop, calls=%fused_computation.3.clone.1 | loop fusion | flops 29360128 | bytes 8912896 | tf_op jit(solution)/shard_map/while/body/eval_jaxpr/reduce_sum | solution.py:24
  251.3 11.7 %add_reduce_fusion.6 = (bf16[128,128,128]{2,1,0:T(8,128)(2,1)S(1)}, bf16[128,128,128]{2,1,0:T(8,128)(2,1)}) fusion(f32[2,128,128]{2,1,0:T(8,128)S(1)} %get-tuple-element.564, f32[2,128,128]{2,1,0:T(8,128)S(1)} %get-tuple-element.566, f32[2,128,128]{2,1,0:T(8,128)S(1)} %get-tuple-element.567, f32[2,128,128]{2,1,0:T(8,128)S(1)} %get-tuple-element.568), kind=kLoop, calls=%fused_computation.3.clone.1 | loop fusion | flops 29360128 | bytes 8912896 | tf_op jit(solution)/shard_map/while/body/eval_jaxpr/reduce_sum | solution.py:24
  310.6 11.7 %add_reduce_fusion.6 = (bf16[128,128,128]{2,1,0:T(8,128)(2,1)S(1)}, bf16[128,128,128]{2,1,0:T(8,128)(2,1)}) fusion(f32[2,128,128]{2,1,0:T(8,128)S(1)} %get-tuple-element.564, f32[2,128,128]{2,1,0:T(8,128)S(1)} %get-tuple-element.566, f32[2,128,128]{2,1,0:T(8,128)S(1)} %get-tuple-element.567, f32[2,128,128]{2,1,0:T(8,128)S(1)} %get-tuple-element.568), kind=kLoop, calls=%fused_computation.3.clone.1 | loop fusion | flops 29360128 | bytes 8912896 | tf_op jit(solution)/shard_map/while/body/eval_jaxpr/reduce_sum | solution.py:24
  340.2 11.7 %add_reduce_fusion.6 = (bf16[128,128,128]{2,1,0:T(8,128)(2,1)S(1)}, bf16[128,128,128]{2,1,0:T(8,128)(2,1)}) fusion(f32[2,128,128]{2,1,0:T(8,128)S(1)} %get-tuple-element.564, f32[2,128,128]{2,1,0:T(8,128)S(1)} %get-tuple-element.566, f32[2,128,128]{2,1,0:T(8,128)S(1)} %get-tuple-element.567, f32[2,128,128]{2,1,0:T(8,128)S(1)} %get-tuple-element.568), kind=kLoop, calls=%fused_computation.3.clone.1 | loop fusion | flops 29360128 | bytes 8912896 | tf_op jit(solution)/shard_map/while/body/eval_jaxpr/reduce_sum | solution.py:24
  369.9 11.7 %add_reduce_fusion.6 = (bf16[128,128,128]{2,1,0:T(8,128)(2,1)S(1)}, bf16[128,128,128]{2,1,0:T(8,128)(2,1)}) fusion(f32[2,128,128]{2,1,0:T(8,128)S(1)} %get-tuple-element.564, f32[2,128,128]{2,1,0:T(8,128)S(1)} %get-tuple-element.566, f32[2,128,128]{2,1,0:T(8,128)S(1)} %get-tuple-element.567, f32[2,128,128]{2,1,0:T(8,128)S(1)} %get-tuple-element.568), kind=kLoop, calls=%fused_computation.3.clone.1 | loop fusion | flops 29360128 | bytes 8912896 | tf_op jit(solution)/shard_map/while/body/eval_jaxpr/reduce_sum | solution.py:24
  399.5 11.7 %add_reduce_fusion.6 = (bf16[128,128,128]{2,1,0:T(8,128)(2,1)S(1)}, bf16[128,128,128]{2,1,0:T(8,128)(2,1)}) fusion(f32[2,128,128]{2,1,0:T(8,128)S(1)} %get-tuple-element.564, f32[2,128,128]{2,1,0:T(8,128)S(1)} %get-tuple-element.566, f32[2,128,128]{2,1,0:T(8,128)S(1)} %get-tuple-element.567, f32[2,128,128]{2,1,0:T(8,128)S(1)} %get-tuple-element.568), kind=kLoop, calls=%fused_computation.3.clone.1 | loop fusion | flops 29360128 | bytes 8912896 | tf_op jit(solution)/shard_map/while/body/eval_jaxpr/reduce_sum | solution.py:24
  460.7 244.2 %while.41 = (s32[]{:T(128)}, f32[64,16384]{1,0:T(8,128)}, s32[8]{0:T(128)S(1)}, s32[]{:T(128)}, bf16[2,2,128,1024]{3,2,1,0:T(8,128)(2,1)}, /*index=5*/bf16[2,2,1...) while((s32[]{:T(128)}, f32[64,16384]{1,0:T(8,128)}, s32[8]{0:T(128)S(1)}, ...), condition=%wide.region_7.9_spmd.clone, body=%wide.region_4.8_spmd.clone.sunk | while | flops 585442176 | bytes 44893884 | solution.py:61
  463.2 11.7 %add_reduce_fusion.7 = (bf16[128,128,128]{2,1,0:T(8,128)(2,1)S(1)}, bf16[128,128,128]{2,1,0:T(8,128)(2,1)}) fusion(f32[2,128,128]{2,1,0:T(8,128)S(1)} %get-tuple-element.580, f32[2,128,128]{2,1,0:T(8,128)S(1)} %get-tuple-element.582, f32[2,128,128]{2,1,0:T(8,128)S(1)} %get-tuple-element.583, f32[2,128,128]{2,1,0:T(8,128)S(1)} %get-tuple-element.584), kind=kLoop, calls=%fused_computation.34.clone.1 | loop fusion | flops 29360128 | bytes 8912896 | tf_op jit(solution)/shard_map/while/body/eval_jaxpr/reduce_sum | solution.py:24
  492.7 11.7 %add_reduce_fusion.7 = (bf16[128,128,128]{2,1,0:T(8,128)(2,1)S(1)}, bf16[128,128,128]{2,1,0:T(8,128)(2,1)}) fusion(f32[2,128,128]{2,1,0:T(8,128)S(1)} %get-tuple-element.580, f32[2,128,128]{2,1,0:T(8,128)S(1)} %get-tuple-element.582, f32[2,128,128]{2,1,0:T(8,128)S(1)} %get-tuple-element.583, f32[2,128,128]{2,1,0:T(8,128)S(1)} %get-tuple-element.584), kind=kLoop, calls=%fused_computation.34.clone.1 | loop fusion | flops 29360128 | bytes 8912896 | tf_op jit(solution)/shard_map/while/body/eval_jaxpr/reduce_sum | solution.py:24
  523.3 11.7 %add_reduce_fusion.7 = (bf16[128,128,128]{2,1,0:T(8,128)(2,1)S(1)}, bf16[128,128,128]{2,1,0:T(8,128)(2,1)}) fusion(f32[2,128,128]{2,1,0:T(8,128)S(1)} %get-tuple-element.580, f32[2,128,128]{2,1,0:T(8,128)S(1)} %get-tuple-element.582, f32[2,128,128]{2,1,0:T(8,128)S(1)} %get-tuple-element.583, f32[2,128,128]{2,1,0:T(8,128)S(1)} %get-tuple-element.584), kind=kLoop, calls=%fused_computation.34.clone.1 | loop fusion | flops 29360128 | bytes 8912896 | tf_op jit(solution)/shard_map/while/body/eval_jaxpr/reduce_sum | solution.py:24
  554.0 11.7 %add_reduce_fusion.7 = (bf16[128,128,128]{2,1,0:T(8,128)(2,1)S(1)}, bf16[128,128,128]{2,1,0:T(8,128)(2,1)}) fusion(f32[2,128,128]{2,1,0:T(8,128)S(1)} %get-tuple-element.580, f32[2,128,128]{2,1,0:T(8,128)S(1)} %get-tuple-element.582, f32[2,128,128]{2,1,0:T(8,128)S(1)} %get-tuple-element.583, f32[2,128,128]{2,1,0:T(8,128)S(1)} %get-tuple-element.584), kind=kLoop, calls=%fused_computation.34.clone.1 | loop fusion | flops 29360128 | bytes 8912896 | tf_op jit(solution)/shard_map/while/body/eval_jaxpr/reduce_sum | solution.py:24
  615.3 11.7 %add_reduce_fusion.7 = (bf16[128,128,128]{2,1,0:T(8,128)(2,1)S(1)}, bf16[128,128,128]{2,1,0:T(8,128)(2,1)}) fusion(f32[2,128,128]{2,1,0:T(8,128)S(1)} %get-tuple-element.580, f32[2,128,128]{2,1,0:T(8,128)S(1)} %get-tuple-element.582, f32[2,128,128]{2,1,0:T(8,128)S(1)} %get-tuple-element.583, f32[2,128,128]{2,1,0:T(8,128)S(1)} %get-tuple-element.584), kind=kLoop, calls=%fused_computation.34.clone.1 | loop fusion | flops 29360128 | bytes 8912896 | tf_op jit(solution)/shard_map/while/body/eval_jaxpr/reduce_sum | solution.py:24
  645.9 11.7 %add_reduce_fusion.7 = (bf16[128,128,128]{2,1,0:T(8,128)(2,1)S(1)}, bf16[128,128,128]{2,1,0:T(8,128)(2,1)}) fusion(f32[2,128,128]{2,1,0:T(8,128)S(1)} %get-tuple-element.580, f32[2,128,128]{2,1,0:T(8,128)S(1)} %get-tuple-element.582, f32[2,128,128]{2,1,0:T(8,128)S(1)} %get-tuple-element.583, f32[2,128,128]{2,1,0:T(8,128)S(1)} %get-tuple-element.584), kind=kLoop, calls=%fused_computation.34.clone.1 | loop fusion | flops 29360128 | bytes 8912896 | tf_op jit(solution)/shard_map/while/body/eval_jaxpr/reduce_sum | solution.py:24
  676.6 11.7 %add_reduce_fusion.7 = (bf16[128,128,128]{2,1,0:T(8,128)(2,1)S(1)}, bf16[128,128,128]{2,1,0:T(8,128)(2,1)}) fusion(f32[2,128,128]{2,1,0:T(8,128)S(1)} %get-tuple-element.580, f32[2,128,128]{2,1,0:T(8,128)S(1)} %get-tuple-element.582, f32[2,128,128]{2,1,0:T(8,128)S(1)} %get-tuple-element.583, f32[2,128,128]{2,1,0:T(8,128)S(1)} %get-tuple-element.584), kind=kLoop, calls=%fused_computation.34.clone.1 | loop fusion | flops 29360128 | bytes 8912896 | tf_op jit(solution)/shard_map/while/body/eval_jaxpr/reduce_sum | solution.py:24
  709.5 243.4 %while.42 = (s32[]{:T(128)}, f32[64,16384]{1,0:T(8,128)}, s32[8]{0:T(128)S(1)}, s32[]{:T(128)}, bf16[2,2,128,1024]{3,2,1,0:T(8,128)(2,1)}, /*index=5*/bf16[2,2,1...) while((s32[]{:T(128)}, f32[64,16384]{1,0:T(8,128)}, s32[8]{0:T(128)S(1)}, ...), condition=%wide.region_11.13_spmd.clone, body=%wide.region_8.12_spmd.clone.sunk | while | flops 585442176 | bytes 44893884 | solution.py:61
  711.9 11.7 %add_reduce_fusion.8 = (bf16[128,128,128]{2,1,0:T(8,128)(2,1)S(1)}, bf16[128,128,128]{2,1,0:T(8,128)(2,1)}) fusion(f32[2,128,128]{2,1,0:T(8,128)S(1)} %get-tuple-element.596, f32[2,128,128]{2,1,0:T(8,128)S(1)} %get-tuple-element.598, f32[2,128,128]{2,1,0:T(8,128)S(1)} %get-tuple-element.599, f32[2,128,128]{2,1,0:T(8,128)S(1)} %get-tuple-element.600), kind=kLoop, calls=%fused_computation.65.clone.1 | loop fusion | flops 29360128 | bytes 8912896 | tf_op jit(solution)/shard_map/while/body/eval_jaxpr/reduce_sum | solution.py:24
  802.4 11.7 %add_reduce_fusion.8 = (bf16[128,128,128]{2,1,0:T(8,128)(2,1)S(1)}, bf16[128,128,128]{2,1,0:T(8,128)(2,1)}) fusion(f32[2,128,128]{2,1,0:T(8,128)S(1)} %get-tuple-element.596, f32[2,128,128]{2,1,0:T(8,128)S(1)} %get-tuple-element.598, f32[2,128,128]{2,1,0:T(8,128)S(1)} %get-tuple-element.599, f32[2,128,128]{2,1,0:T(8,128)S(1)} %get-tuple-element.600), kind=kLoop, calls=%fused_computation.65.clone.1 | loop fusion | flops 29360128 | bytes 8912896 | tf_op jit(solution)/shard_map/while/body/eval_jaxpr/reduce_sum | solution.py:24
  833.0 11.7 %add_reduce_fusion.8 = (bf16[128,128,128]{2,1,0:T(8,128)(2,1)S(1)}, bf16[128,128,128]{2,1,0:T(8,128)(2,1)}) fusion(f32[2,128,128]{2,1,0:T(8,128)S(1)} %get-tuple-element.596, f32[2,128,128]{2,1,0:T(8,128)S(1)} %get-tuple-element.598, f32[2,128,128]{2,1,0:T(8,128)S(1)} %get-tuple-element.599, f32[2,128,128]{2,1,0:T(8,128)S(1)} %get-tuple-element.600), kind=kLoop, calls=%fused_computation.65.clone.1 | loop fusion | flops 29360128 | bytes 8912896 | tf_op jit(solution)/shard_map/while/body/eval_jaxpr/reduce_sum | solution.py:24
  863.6 11.7 %add_reduce_fusion.8 = (bf16[128,128,128]{2,1,0:T(8,128)(2,1)S(1)}, bf16[128,128,128]{2,1,0:T(8,128)(2,1)}) fusion(f32[2,128,128]{2,1,0:T(8,128)S(1)} %get-tuple-element.596, f32[2,128,128]{2,1,0:T(8,128)S(1)} %get-tuple-element.598, f32[2,128,128]{2,1,0:T(8,128)S(1)} %get-tuple-element.599, f32[2,128,128]{2,1,0:T(8,128)S(1)} %get-tuple-element.600), kind=kLoop, calls=%fused_computation.65.clone.1 | loop fusion | flops 29360128 | bytes 8912896 | tf_op jit(solution)/shard_map/while/body/eval_jaxpr/reduce_sum | solution.py:24
  894.1 11.7 %add_reduce_fusion.8 = (bf16[128,128,128]{2,1,0:T(8,128)(2,1)S(1)}, bf16[128,128,128]{2,1,0:T(8,128)(2,1)}) fusion(f32[2,128,128]{2,1,0:T(8,128)S(1)} %get-tuple-element.596, f32[2,128,128]{2,1,0:T(8,128)S(1)} %get-tuple-element.598, f32[2,128,128]{2,1,0:T(8,128)S(1)} %get-tuple-element.599, f32[2,128,128]{2,1,0:T(8,128)S(1)} %get-tuple-element.600), kind=kLoop, calls=%fused_computation.65.clone.1 | loop fusion | flops 29360128 | bytes 8912896 | tf_op jit(solution)/shard_map/while/body/eval_jaxpr/reduce_sum | solution.py:24
  924.7 11.7 %add_reduce_fusion.8 = (bf16[128,128,128]{2,1,0:T(8,128)(2,1)S(1)}, bf16[128,128,128]{2,1,0:T(8,128)(2,1)}) fusion(f32[2,128,128]{2,1,0:T(8,128)S(1)} %get-tuple-element.596, f32[2,128,128]{2,1,0:T(8,128)S(1)} %get-tuple-element.598, f32[2,128,128]{2,1,0:T(8,128)S(1)} %get-tuple-element.599, f32[2,128,128]{2,1,0:T(8,128)S(1)} %get-tuple-element.600), kind=kLoop, calls=%fused_computation.65.clone.1 | loop fusion | flops 29360128 | bytes 8912896 | tf_op jit(solution)/shard_map/while/body/eval_jaxpr/reduce_sum | solution.py:24
  967.2 42.6 %reduce-scatter.5.cloned.1.call-done = bf16[8,49152]{1,0:T(8,128)(2,1)} async-done(((bf16[64,49152]{1,0:T(8,128)(2,1)}), bf16[8,49152]{1,0:T(8,128)(2,1)}) %reduce-scatter.5.cloned.1.call-update) | async-done | bytes 786448
  (301 shorter events, 525.5 us)
Async XLA Ops:
  6.5 203.4 %all-gather.2.cloned.1.call-start = ((), (), s32[]{:S(2)}) async-start(), calls=%async_computation.1 | async-start | bytes 35651584 | tf_op jit(solution)/shard_map/all_gather | solution.py:70
  7.3 1002.5 %reduce-scatter.5.cloned.1.call-start = ((), (), s32[]{:S(2)}) async-start(), calls=%async_computation.2 | async-start | bytes 7077888
  952.9 3.5 copy-start
Sparse Core Ops, SparseCore 0:
  9.5 200.4 all-gather.1
  967.3 42.4 reduce-scatter.4
where the time goes:
time: 1020 us
  other arithmetic  475 us (47%)
  waiting for transfers between devices  231 us (23%)
  matrix products  218 us (21%)
  local copies, waits for them, and re-layouts  53.4 us (5%)
  between operations  25.5 us (2%)
  loops' own time  16.6 us (2%)
    reduce_sum x24, other arithmetic, cross_block(): jnp.sum(left_wide[:, 0, :, None, :] * right_wide[:, 0, None, :, :] + left...  280 us
    dot_general x24, matrix products, block_step(): lax.dot_general(phases, stacked, (((0,), (1,)), ((), ())), preferred_elem...  218 us
    all_gather x1, waiting for transfers between devices, per_device(): shards = lax.all_gather(spectra, 'tiles', axis=0, tiled=True)  187 us
    concatenate x24, other arithmetic, cross_block(): jnp.concatenate([real_part, imag_part], axis=-1)  171 us
    unnamed x3, waiting for transfers between devices  43.3 us
  transfers between devices with their start and end apart: 2, of which 2 were waited for; matrix products, arithmetic and copies ran while one was open for 0% of the time, Pallas kernels for 0%

commit v1 on v0

--- a/solution.py
+++ b/solution.py
@@ -67,7 +67,9 @@
     own_index = lax.axis_index("tiles")
     wanted = lax.dynamic_index_in_dim(requests, own_index, 0, keepdims=False)
     empty = jnp.zeros((wanted.shape[0],) + spectra.shape[1:], jnp.bfloat16)
-    shards = lax.all_gather(spectra, "tiles", axis=0, tiled=True)
+    shards = jnp.concatenate(
+        lax.all_to_all(jnp.stack([spectra] * lax.axis_size("tiles")), "tiles", 0, 0), axis=0
+    )
     inside = (wanted >= 0) & (wanted < shards.shape[0])
     taken = jnp.take(shards, jnp.clip(wanted, 0, shards.shape[0] - 1), axis=0)
     needed = jnp.where(inside[:, None, None, None, None], taken, empty)

time: 1020 us -> 1460 us (1.43)
  waiting for transfers between devices: 231 us -> 654 us
    all_to_all x0 -> x1, waiting for transfers between devices: none -> 606 us  [per_device(): lax.all_to_all(jnp.stack([spectra] * lax.axis_size('tiles')), 'tiles', 0, 0)]
    all_gather x1 -> x0, waiting for transfers between devices: 187 us -> none  [per_device(): shards = lax.all_gather(spectra, 'tiles', axis=0, tiled=True)]
    unnamed x3 -> x2, waiting for transfers between devices: 43.3 us -> 47.9 us
where the time goes in v1:
time: 1460 us
  waiting for transfers between devices  654 us (45%)
  other arithmetic  473 us (32%)
  matrix products  217 us (15%)
  local copies, waits for them, and re-layouts  63.3 us (4%)
  between operations  25.8 us (2%)
  loops' own time  15 us (1%)
    all_to_all x1, waiting for transfers between devices, per_device(): lax.all_to_all(jnp.stack([spectra] * lax.axis_size('tiles')), 'tiles', 0, 0)  606 us
    reduce_sum x24, other arithmetic, cross_block(): jnp.sum(left_wide[:, 0, :, None, :] * right_wide[:, 0, None, :, :] + left...  280 us
    dot_general x24, matrix products, block_step(): lax.dot_general(phases, stacked, (((0,), (1,)), ((), ())), preferred_elem...  217 us
    concatenate x24, other arithmetic, cross_block(): jnp.concatenate([real_part, imag_part], axis=-1)  170 us
    unnamed x2, waiting for transfers between devices  47.9 us
  transfers between devices with their start and end apart: 2, of which 2 were waited for; matrix products, arithmetic and copies ran while one was open for 0% of the time, Pallas kernels for 0%

profile of v1, /device:TPU:1, one launch (start us, length us, event | category | flops | bytes accessed | tf_op | source)
XLA Modules:
  0.0 1457.1 jit_solution(6158072131427987901)
XLA Ops:
  6.5 12.2 stack.10
  40.9 606.3 %all-to-all-done = bf16[16,2,2,2,128,1024]{5,4,3,2,1,0:T(8,128)(2,1)} async-done(((bf16[16,2,2,2,128,1024]{5,4,3,2,1,0:T(8,128)(2,1)}), bf16[16,2,2,2,128,1024]{5,4,3,2,1,0:T(8,128)(2,1)}, u32[]{:S(2)}, u32[]{:S(2)}) %all-to-all-start) | async-done | bytes 33554464 | tf_op jit(solution)/shard_map/all_to_all | solution.py:71
  658.6 234.8 %while.40 = (s32[]{:T(128)}, f32[64,16384]{1,0:T(8,128)}, s32[8]{0:T(128)S(1)}, s32[]{:T(128)}, bf16[2,2,128,1024]{3,2,1,0:T(8,128)(2,1)S(1)}, /*index=5*/bf16[2...) while((s32[]{:T(128)}, f32[64,16384]{1,0:T(8,128)}, ...), condition=%wide.region_3.5_spmd.clone, body=%wide.region_0.0_spmd.clone.sunk | while | flops 585442176 | bytes 44893884 | solution.py:61
  659.9 11.6 add_reduce_fusion.6
  688.2 11.6 add_reduce_fusion.6
  747.2 11.6 add_reduce_fusion.6
  776.7 11.6 add_reduce_fusion.6
  835.7 11.6 add_reduce_fusion.6
  865.2 11.6 add_reduce_fusion.6
  896.7 241.9 %while.41 = (s32[]{:T(128)}, f32[64,16384]{1,0:T(8,128)}, s32[8]{0:T(128)S(1)}, s32[]{:T(128)}, bf16[2,2,128,1024]{3,2,1,0:T(8,128)(2,1)}, /*index=5*/bf16[2,2,1...) while((s32[]{:T(128)}, f32[64,16384]{1,0:T(8,128)}, s32[8]{0:T(128)S(1)}, ...), condition=%wide.region_7.9_spmd.clone, body=%wide.region_4.8_spmd.clone.sunk | while | flops 585442176 | bytes 44893884 | solution.py:61
  899.1 11.6 add_reduce_fusion.7
  928.3 11.6 add_reduce_fusion.7
  958.6 11.6 add_reduce_fusion.7
  989.0 11.6 add_reduce_fusion.7
  1019.4 11.6 add_reduce_fusion.7
  1080.1 11.6 add_reduce_fusion.7
  1110.4 11.6 add_reduce_fusion.7
  1143.2 242.3 %while.42 = (s32[]{:T(128)}, f32[64,16384]{1,0:T(8,128)}, s32[8]{0:T(128)S(1)}, s32[]{:T(128)}, bf16[2,2,128,1024]{3,2,1,0:T(8,128)(2,1)}, /*index=5*/bf16[2,2,1...) while((s32[]{:T(128)}, f32[64,16384]{1,0:T(8,128)}, s32[8]{0:T(128)S(1)}, ...), condition=%wide.region_11.13_spmd.clone, body=%wide.region_8.12_spmd.clone.sunk | while | flops 585442176 | bytes 44893884 | solution.py:61
  1145.5 11.6 add_reduce_fusion.8
  1174.7 11.6 add_reduce_fusion.8
  1205.2 11.6 add_reduce_fusion.8
  1235.6 11.6 add_reduce_fusion.8
  1326.9 11.6 add_reduce_fusion.8
  1399.8 47.9 %reduce-scatter.5.cloned.1.call-done = bf16[8,49152]{1,0:T(8,128)(2,1)} async-done(((bf16[64,49152]{1,0:T(8,128)(2,1)}), bf16[8,49152]{1,0:T(8,128)(2,1)}) %reduce-scatter.5.cloned.1.call-update) | async-done | bytes 786448
  (305 shorter events, 540.2 us)
Async XLA Ops:
  18.7 8.9 copy-start.2
  18.7 21.8 %copy-start.1 = (s32[16,6]{0,1:T(8,128)S(1)}, s32[16,6]{0,1:T(8,128)}, u32[]{:S(2)}) copy-start(s32[16,6]{0,1:T(8,128)} %param.13) | copy-start | bytes 1156
  18.7 628.5 %all-to-all-start = ((bf16[16,2,2,2,128,1024]{5,4,3,2,1,0:T(8,128)(2,1)}), bf16[16,2,2,2,128,1024]{5,4,3,2,1,0:T(8,128)(2,1)}, u32[]{:S(2)}, u32[]{:S(2)}) async-start(bf16[16,2,2,2,128,1024]{5,4,3,2,1,0:T(8,128)(2,1)} %stack.10), calls=%async_computation | async-start | bytes 67108864 | tf_op jit(solution)/shard_map/all_to_all | solution.py:71
  27.5 1420.1 %reduce-scatter.5.cloned.1.call-start = ((), (), s32[]{:S(2)}) async-start(), calls=%async_computation.2 | async-start | bytes 7077888
  1385.5 3.5 copy-start
Sparse Core Ops, SparseCore 0:
  1399.9 47.7 reduce-scatter.4
